TPU v7x, 32 devices: a whole 2x2x4 slice. The times are simulated.
32 devices in a mesh: dp: 8 (over z, x), ctx: 4 (over y, core).
Axes of the slice: x: 2, y: 2, z: 4, core: 2. Of those that a mesh axis runs over, the one named last changes fastest.
Arguments:
- states: bfloat16 [32, 1024, 960], P('dp', 'ctx'), may hold values from -6 to 6
- teacher: bfloat16 [32, 1024, 960], P('dp', 'ctx'), may hold values from -6 to 6
- validity: int32 [32, 1024], P('dp', 'ctx'), may hold values from 0 to 1, as said below
- chosen: int32 [32, 1024], P('dp', 'ctx'), may hold values from 0 to 1, as said below
- attn_pack: bfloat16 [960, 2560], P(None, ('dp', 'ctx')), may hold values from -1 to 1
- gate_up: bfloat16 [960, 5120], P(None, ('dp', 'ctx')), may hold values from -0.1875 to 0.1875
- down_proj: bfloat16 [960, 2560], P(None, ('dp', 'ctx')), may hold values from -0.125 to 0.125
- norm_gains: float32 [2, 960], replicated, may hold values from 0.25 to 1.75
- router: float32 [960], replicated, may hold values from -0.12 to 0.12
Outputs:
- states_out: bfloat16 [32, 1024, 960], P('dp', 'ctx')
- mse_loss: float32 [], replicated
- states_grad: float32 [32, 1024, 960], P('dp', 'ctx')
- attn_pack_grad: float32 [960, 2560], P(None, ('dp', 'ctx'))
- gate_up_grad: float32 [960, 5120], P(None, ('dp', 'ctx'))
- down_proj_grad: float32 [960, 2560], P(None, ('dp', 'ctx'))
- norm_gains_grad: float32 [2, 960], replicated
- router_grad: float32 [960], replicated
Inputs may be any that keep to these rules, and one draw needn't show every extreme that they name: `validity`: the first token of every sequence is valid. `chosen`: each sequence has 640 or 641 selected tokens, the first token always among them.
All inputs are finite; a program needn't handle non-finite values.
Results may differ from a plain program's by a relative error of at most 0.012.
Values may be sent and summed in bfloat16 or wider, within the bound.
No kernel may reach another device: no remote copies, remote signals or barrier semaphores. Data moves between devices by JAX's collectives and lax.ppermute only.
A program may use at most 320 MiB of HBM per device.

v0:
```python
import jax
import jax.numpy as jnp
from jax import lax
from jax.sharding import PartitionSpec as P

D = 960
HEADS = 15
KV_HEADS = 5
HEAD = 64
FF = 2560
MICRO = 2
EPS = 1e-05
THETA = 10000.0


def shortened(x):
    return jax.tree.map(lambda a: a.astype(jnp.bfloat16) if a.dtype == jnp.float32 else a, x)


def rope_tables(positions):
    half_head = HEAD // 2
    freqs = THETA ** (-(jnp.arange(half_head).astype(jnp.float32) * 2.0 / HEAD))
    angles = positions.astype(jnp.float32)[:, None] * freqs[None, :]
    return (jnp.cos(angles)[:, None, :], jnp.sin(angles)[:, None, :])


def rotate(values, cosine, sine):
    half_head = HEAD // 2
    first = values[..., :half_head]
    second = values[..., half_head:]
    return jnp.concatenate(
        [first * cosine - second * sine, second * cosine + first * sine], axis=-1
    )


def rotate_back(values, cosine, sine):
    half_head = HEAD // 2
    first = values[..., :half_head]
    second = values[..., half_head:]
    return jnp.concatenate(
        [first * cosine + second * sine, second * cosine - first * sine], axis=-1
    )


def norm_back(grad_out, values, inv_rms, gain_row):
    scaled = grad_out * gain_row
    return inv_rms * scaled - values * inv_rms**3 * jnp.mean(
        scaled * values, axis=-1, keepdims=True
    )


def scores_of(queries, keys, allowed):
    scores = (
        jnp.einsum("bqgrh,bkgh->bgrqk", queries, keys, preferred_element_type=jnp.float32) * 0.125
    )
    return jnp.where(allowed, scores, -jnp.inf)


def over_rows(left, right):
    return lax.dot_general(
        left, right, (((0, 1), (0, 1)), ((), ())), preferred_element_type=jnp.float32
    )


def by_columns(left, right):
    return lax.dot_general(
        left, right, (((2,), (1,)), ((), ())), preferred_element_type=jnp.float32
    )


def on_device(states, teacher, validity, chosen, attn_pack, gate_up, down_proj, norm_gains, router):
    seq_count, block_rows, width = states.shape
    seq_micro = seq_count // MICRO
    ctx_count = lax.axis_size("ctx")
    dp_count = lax.axis_size("dp")
    ctx_spot = lax.axis_index("ctx")
    seq_length = block_rows * ctx_count
    qkv_cols = D + 2 * KV_HEADS * HEAD
    kv_width = KV_HEADS * HEAD
    per_kv = HEADS // KV_HEADS
    cosine, sine = rope_tables(ctx_spot * block_rows + jnp.arange(block_rows))
    early_block = jnp.arange(seq_length) // block_rows <= ctx_spot
    valid_all = validity.astype(jnp.float32)
    chosen_all = chosen.astype(jnp.float32)
    key_flags = (validity * chosen).astype(jnp.bfloat16)
    gain_one = norm_gains[0]
    gain_two = norm_gains[1]
    packs = (attn_pack, gate_up, down_proj)
    valid_total = lax.psum(jnp.sum(valid_all), ("dp", "ctx"))
    grad_attn = jnp.zeros((D, qkv_cols + D), jnp.float32)
    grad_gu = jnp.zeros((D, 2 * FF), jnp.float32)
    grad_down = jnp.zeros((D, FF), jnp.float32)
    grad_gain_one = jnp.zeros((D,), jnp.float32)
    grad_gain_two = jnp.zeros((D,), jnp.float32)
    grad_router = jnp.zeros((D,), jnp.float32)
    energy = jnp.zeros((), jnp.float32)
    out_parts = []
    input_grads = []
    for micro_index in range(MICRO):
        lower = micro_index * seq_micro
        upper = lower + seq_micro
        x_float = states[lower:upper].astype(jnp.float32)
        teacher_rows = teacher[lower:upper].astype(jnp.float32)
        valid_rows = valid_all[lower:upper]
        chosen_rows = chosen_all[lower:upper]
        fresh = (
            lax.all_gather(packs[0], ("dp", "ctx"), axis=1, tiled=True),
            lax.all_gather(packs[1], ("dp", "ctx"), axis=1, tiled=True),
            lax.all_gather(packs[2], ("dp", "ctx"), axis=1, tiled=True),
        )
        w_attn, w_gu, w_down = fresh
        inv_one = lax.rsqrt(jnp.mean(x_float * x_float, axis=-1, keepdims=True) + EPS)
        normed = (x_float * inv_one * gain_one).astype(jnp.bfloat16)
        mixed = jnp.dot(normed, w_attn[:, :qkv_cols], preferred_element_type=jnp.float32)
        queries = mixed[..., :D].reshape(seq_micro, block_rows, HEADS, HEAD)
        keys = mixed[..., D : D + kv_width].reshape(seq_micro, block_rows, KV_HEADS, HEAD)
        values_in = mixed[..., D + kv_width :].reshape(seq_micro, block_rows, KV_HEADS, HEAD)
        rot_queries = (
            rotate(queries, cosine, sine)
            .astype(jnp.bfloat16)
            .reshape(seq_micro, block_rows, KV_HEADS, per_kv, HEAD)
        )
        rot_keys = rotate(keys, cosine, sine).astype(jnp.bfloat16)
        value_low = values_in.astype(jnp.bfloat16)
        keys_all, values_all, flags_all = (
            lax.all_gather(rot_keys, "ctx", axis=1, tiled=True),
            lax.all_gather(value_low, "ctx", axis=1, tiled=True),
            lax.all_gather(key_flags[lower:upper], "ctx", axis=1, tiled=True),
        )
        allowed = (early_block[None, :] & (flags_all > 0.5))[:, None, None, None, :]
        scores = scores_of(rot_queries, keys_all, allowed)
        row_max = jnp.max(scores, axis=-1, keepdims=True)
        expd = jnp.exp(scores - row_max)
        row_total = jnp.sum(expd, axis=-1, keepdims=True)
        log_total = row_max + jnp.log(row_total)
        probs_low = (expd / row_total).astype(jnp.bfloat16)
        heads_out = jnp.einsum(
            "bgrqk,bkgh->bqgrh", probs_low, values_all, preferred_element_type=jnp.float32
        )
        heads_low = heads_out.reshape(seq_micro, block_rows, D).astype(jnp.bfloat16)
        attn_out = by_columns(heads_low, w_attn[:, qkv_cols:])
        inner = x_float + attn_out
        inv_two = lax.rsqrt(jnp.mean(inner * inner, axis=-1, keepdims=True) + EPS)
        normed_two = (inner * inv_two * gain_two).astype(jnp.bfloat16)
        gate_both = jnp.dot(normed_two, w_gu, preferred_element_type=jnp.float32)
        gate_part = gate_both[..., :FF]
        up_part = gate_both[..., FF:]
        gate_sig = jax.nn.sigmoid(gate_part)
        hidden = (gate_part * gate_sig * up_part).astype(jnp.bfloat16)
        ffn_out = by_columns(hidden, w_down)
        gate_prob = jax.nn.sigmoid(jnp.dot(x_float, router, precision=lax.Precision.HIGHEST))
        weight_mix = chosen_rows * gate_prob
        branch = attn_out + ffn_out
        result = x_float + weight_mix[..., None] * branch
        out_parts.append(result.astype(jnp.bfloat16))
        diff = valid_rows[..., None] * (result - teacher_rows)
        energy = energy + 0.5 * jnp.sum(diff * diff)
        w_attn, w_gu, w_down = (
            lax.all_gather(packs[0], ("dp", "ctx"), axis=1, tiled=True),
            lax.all_gather(packs[1], ("dp", "ctx"), axis=1, tiled=True),
            lax.all_gather(packs[2], ("dp", "ctx"), axis=1, tiled=True),
        )
        d_branch = weight_mix[..., None] * diff
        d_logit = chosen_rows * jnp.sum(diff * branch, axis=-1) * gate_prob * (1.0 - gate_prob)
        grad_router = grad_router + jnp.einsum(
            "bt,btd->d", d_logit, x_float, precision=lax.Precision.HIGHEST
        )
        d_states = diff + d_logit[..., None] * router
        d_ffn = d_branch.astype(jnp.bfloat16)
        d_hidden = jnp.dot(d_ffn, w_down, preferred_element_type=jnp.float32)
        grad_down = grad_down + over_rows(d_ffn, hidden)
        d_gate = d_hidden * up_part * gate_sig * (1.0 + gate_part * (1.0 - gate_sig))
        d_up = d_hidden * gate_part * gate_sig
        d_gu_low = jnp.concatenate([d_gate, d_up], axis=-1).astype(jnp.bfloat16)
        d_normed_two = by_columns(d_gu_low, w_gu)
        grad_gu = grad_gu + over_rows(normed_two, d_gu_low)
        grad_gain_two = grad_gain_two + jnp.sum(d_normed_two * inner * inv_two, axis=(0, 1))
        d_inner = norm_back(d_normed_two, inner, inv_two, gain_two)
        d_states = d_states + d_inner
        d_attn_low = (d_branch + d_inner).astype(jnp.bfloat16)
        d_heads = jnp.dot(d_attn_low, w_attn[:, qkv_cols:], preferred_element_type=jnp.float32)
        d_heads_low = d_heads.astype(jnp.bfloat16).reshape(
            seq_micro, block_rows, KV_HEADS, per_kv, HEAD
        )
        grad_out_proj = over_rows(d_attn_low, heads_low)
        probs = jnp.exp(scores_of(rot_queries, keys_all, allowed) - log_total)
        d_probs = jnp.einsum(
            "bqgrh,bkgh->bgrqk", d_heads_low, values_all, preferred_element_type=jnp.float32
        )
        d_scores = (probs * (d_probs - jnp.sum(probs * d_probs, axis=-1, keepdims=True))).astype(
            jnp.bfloat16
        )
        d_queries = (
            jnp.einsum("bgrqk,bkgh->bqgrh", d_scores, keys_all, preferred_element_type=jnp.float32)
            * 0.125
        )
        d_keys_all = (
            jnp.einsum(
                "bgrqk,bqgrh->bkgh", d_scores, rot_queries, preferred_element_type=jnp.float32
            )
            * 0.125
        )
        d_values_all = jnp.einsum(
            "bgrqk,bqgrh->bkgh",
            probs.astype(jnp.bfloat16),
            d_heads_low,
            preferred_element_type=jnp.float32,
        )
        d_keys, d_values = (
            lax.psum_scatter(
                d_keys_all.astype(jnp.bfloat16), "ctx", scatter_dimension=1, tiled=True
            ).astype(jnp.float32),
            lax.psum_scatter(
                d_values_all.astype(jnp.bfloat16), "ctx", scatter_dimension=1, tiled=True
            ).astype(jnp.float32),
        )
        d_queries = rotate_back(d_queries.reshape(seq_micro, block_rows, HEADS, HEAD), cosine, sine)
        d_keys = rotate_back(d_keys, cosine, sine)
        d_mixed = jnp.concatenate(
            [
                d_queries.reshape(seq_micro, block_rows, D),
                d_keys.reshape(seq_micro, block_rows, kv_width),
                d_values.reshape(seq_micro, block_rows, kv_width),
            ],
            axis=-1,
        ).astype(jnp.bfloat16)
        d_normed = by_columns(d_mixed, w_attn[:, :qkv_cols])
        grad_attn = grad_attn + jnp.concatenate([over_rows(normed, d_mixed), grad_out_proj], axis=1)
        grad_gain_one = grad_gain_one + jnp.sum(d_normed * x_float * inv_one, axis=(0, 1))
        d_states = d_states + norm_back(d_normed, x_float, inv_one, gain_one)
        input_grads.append(d_states)

    def owner_layout(grad_whole):
        return grad_whole.reshape(
            D, dp_count, ctx_count, grad_whole.shape[1] // (dp_count * ctx_count)
        )

    by_ctx = (
        lax.all_to_all(
            owner_layout(grad_attn).astype(jnp.bfloat16),
            "ctx",
            split_axis=2,
            concat_axis=2,
            tiled=True,
        ).astype(jnp.float32),
        lax.all_to_all(
            owner_layout(grad_gu).astype(jnp.bfloat16),
            "ctx",
            split_axis=2,
            concat_axis=2,
            tiled=True,
        ).astype(jnp.float32),
        lax.all_to_all(
            owner_layout(grad_down).astype(jnp.bfloat16),
            "ctx",
            split_axis=2,
            concat_axis=2,
            tiled=True,
        ).astype(jnp.float32),
    )
    attn_ctx, gu_ctx, down_ctx = [jnp.sum(piece, axis=2) for piece in by_ctx]
    by_dp = (
        lax.all_to_all(shortened(attn_ctx), "dp", split_axis=1, concat_axis=1, tiled=True).astype(
            attn_ctx.dtype
        ),
        lax.all_to_all(shortened(gu_ctx), "dp", split_axis=1, concat_axis=1, tiled=True).astype(
            gu_ctx.dtype
        ),
        lax.all_to_all(shortened(down_ctx), "dp", split_axis=1, concat_axis=1, tiled=True).astype(
            down_ctx.dtype
        ),
    )
    attn_grad_part, gu_grad_part, down_grad_part = [jnp.sum(piece, axis=1) for piece in by_dp]
    grad_gains = jnp.stack([grad_gain_one, grad_gain_two], axis=0)
    energy_all, gains_all, router_all = lax.psum((energy, grad_gains, grad_router), ("dp", "ctx"))
    mse_loss = 2.0 * energy_all / (valid_total * D)
    return (
        jnp.concatenate(out_parts, axis=0),
        mse_loss,
        jnp.concatenate(input_grads, axis=0),
        attn_grad_part,
        gu_grad_part,
        down_grad_part,
        gains_all,
        router_all,
    )


def solution(mesh):
    placed = (
        P("dp", "ctx", None),
        P("dp", "ctx", None),
        P("dp", "ctx"),
        P("dp", "ctx"),
        P(None, ("dp", "ctx")),
        P(None, ("dp", "ctx")),
        P(None, ("dp", "ctx")),
        P(),
        P(),
    )
    return jax.shard_map(
        on_device,
        mesh=mesh,
        in_specs=placed,
        out_specs=(
            P("dp", "ctx", None),
            P(),
            P("dp", "ctx", None),
            P(None, ("dp", "ctx")),
            P(None, ("dp", "ctx")),
            P(None, ("dp", "ctx")),
            P(),
            P(),
        ),
        check_vma=False,
    )
```

profile of v0, /device:TPU:0, one launch (start us, length us, event | category | flops | bytes accessed | tf_op | source)
XLA Modules:
  0.0 1026.9 jit_solution(13568377429993740406)
XLA Ops:
  10.8 68.1 %all-gather.8.cloned.1.call-done = bf16[960,2560]{0,1:T(8,128)(2,1)} async-done(((bf16[960,80]{0,1:T(8,128)(2,1)}), bf16[960,2560]{0,1:T(8,128)(2,1)}) %all-gather.8.cloned.1.call-update) | async-done | bytes 4915216 | tf_op jit(solution)/shard_map/all_gather | solution.py:107
  110.5 15.0 %bitcast_reduce_fusion = (f32[2,5,3,256]{3,2,1,0:T(4,128)S(1)}, f32[2,5,1024,256,3]{3,2,4,1,0:T(8,128)}) fusion(bf16[2,256,5,3,32]{1,4,3,2,0:T(8,128)(2,1)S(1)} %bitcast.322, bf16[2,256,5,3,32]{1,4,3,2,0:T(8,128)(2,1)} %bitcast.324, bf16[2,1024,5,64]{1,3,2,0:T(8,128)(2,1)} %all-gather.20.cloned.1.call-done, pred[2,1024]{1,0:T(4,128)(4,1)S(1)} %get-tuple-element.98), kind=kOutput, calls=%fused_computation.12 | convolution fusion | flops 1032184320 | bytes 33783808 | tf_op jit(solution)/shard_map/bqgrh,bkgh->bgrqk/dot_general | solution.py:54
  125.5 13.0 %fusion.11 = f32[2,5,3,256]{3,2,1,0:T(4,128)S(1)} fusion(f32[2,5,1024,256,3]{3,2,4,1,0:T(8,128)} %get-tuple-element.100, f32[2,5,3,256]{3,2,1,0:T(4,128)S(1)} %get-tuple-element.99), kind=kLoop, calls=%fused_computation.25 | loop fusion | flops 15720960 | bytes 31518720 | tf_op jit(solution)/shard_map/reduce_sum | solution.py:134
  138.5 14.3 %bitcast_reduce_fusion.1 = (f32[2,5,3,256]{3,2,1,0:T(4,128)S(1)}, f32[2,5,1024,256,3]{3,2,4,1,0:T(8,128)}) fusion(bf16[2,256,5,3,32]{1,4,3,2,0:T(8,128)(2,1)S(1)} %bitcast.320, bf16[2,256,5,3,32]{1,4,3,2,0:T(8,128)(2,1)S(1)} %bitcast.318, bf16[2,1024,5,64]{1,3,2,0:T(8,128)(2,1)} %all-gather.12.cloned.1.call-done, pred[2,1024]{1,0:T(4,128)(4,1)S(1)} %get-tuple-element.97), kind=kOutput, calls=%fused_computation.17 | convolution fusion | flops 1032184320 | bytes 33783808 | tf_op jit(solution)/shard_map/bqgrh,bkgh->bgrqk/dot_general | solution.py:54
  152.8 13.1 %fusion.10 = f32[2,5,3,256]{3,2,1,0:T(4,128)S(1)} fusion(f32[2,5,1024,256,3]{3,2,4,1,0:T(8,128)} %get-tuple-element.102, f32[2,5,3,256]{3,2,1,0:T(4,128)S(1)} %get-tuple-element.101), kind=kLoop, calls=%fused_computation.24 | loop fusion | flops 15720960 | bytes 31518720 | tf_op jit(solution)/shard_map/reduce_sum | solution.py:134
  166.0 13.3 %fusion.72 = bf16[2,5,64,3,256]{4,2,3,1,0:T(8,128)(2,1)S(1)} fusion(f32[2,5,1024,256,3]{3,2,4,1,0:T(8,128)} %get-tuple-element.100, f32[2,5,3,256]{3,2,1,0:T(4,128)S(1)} %fusion.11, f32[2,5,3,256]{3,2,1,0:T(4,128)S(1)} %get-tuple-element.99, bf16[2,1024,5,64]{1,3,2,0:T(8,128)(2,1)} %all-gather.18.cloned.1.call-done), kind=kOutput, calls=%fused_computation.144 | convolution fusion | flops 1030717440 | bytes 33812480 | tf_op jit(solution)/shard_map/bgrqk,bkgh->bqgrh/dot_general | solution.py:137
  183.7 13.5 %fusion.73 = bf16[2,5,64,3,256]{4,2,3,1,0:T(8,128)(2,1)S(1)} fusion(f32[2,5,1024,256,3]{3,2,4,1,0:T(8,128)} %get-tuple-element.102, f32[2,5,3,256]{3,2,1,0:T(4,128)S(1)} %fusion.10, f32[2,5,3,256]{3,2,1,0:T(4,128)S(1)} %get-tuple-element.101, bf16[2,1024,5,64]{1,3,2,0:T(8,128)(2,1)} %all-gather.10.cloned.1.call-done), kind=kOutput, calls=%fused_computation.145 | convolution fusion | flops 1030717440 | bytes 33812480 | tf_op jit(solution)/shard_map/bgrqk,bkgh->bqgrh/dot_general | solution.py:137
  203.7 50.6 %all-gather.14.cloned.1.call-done = bf16[960,5120]{0,1:T(8,128)(2,1)} async-done(((bf16[960,160]{0,1:T(8,128)(2,1)}), bf16[960,5120]{0,1:T(8,128)(2,1)}) %all-gather.14.cloned.1.call-update) | async-done | bytes 9830416 | tf_op jit(solution)/shard_map/all_gather | solution.py:108
  254.3 9.5 fusion.27
  284.5 36.5 %all-gather.16.cloned.1.call-done = bf16[960,2560]{0,1:T(8,128)(2,1)} async-done(((bf16[960,80]{0,1:T(8,128)(2,1)}), bf16[960,2560]{0,1:T(8,128)(2,1)}) %all-gather.16.cloned.1.call-update) | async-done | bytes 4915216 | tf_op jit(solution)/shard_map/all_gather | solution.py:109
  329.1 10.3 multiply_reduce_fusion.3
  339.4 11.5 %multiply_convert_fusion.3 = (bf16[2,256,2560]{2,1,0:T(8,128)(2,1)S(1)}, bf16[2,256,2560]{2,1,0:T(8,128)(2,1)}) fusion(f32[2,256,5120]{2,1,0:T(8,128)} %copy-done.6, bf16[960,2560]{0,1:T(8,128)(2,1)} %all-gather.16.cloned.1.call-done, f32[2,256,960]{1,2,0:T(8,128)S(1)} %get-tuple-element.43, f32[2,256]{1,0:T(2,128)S(1)} %copy-done.48), kind=kOutput, calls=%fused_computation.62 | convolution fusion | flops 2534604800 | bytes 22611968 | tf_op jit(solution)/shard_map/dot_general | solution.py:170
  350.9 10.2 multiply_convert_fusion.1
  361.1 13.9 %fusion.25 = f32[2,256,960]{1,2,0:T(8,128)} fusion(bf16[960,5120]{0,1:T(8,128)(2,1)} %all-gather.14.cloned.1.call-done, bf16[2,256,2560]{2,1,0:T(8,128)(2,1)} %get-tuple-element.37, bf16[2,256,2560]{2,1,0:T(8,128)(2,1)S(1)} %get-tuple-element.36), kind=kOutput, calls=%fused_computation.38 | convolution fusion | flops 5043650560 | bytes 17039360 | tf_op jit(solution)/shard_map/dot_general | solution.py:66
  375.0 15.0 %multiply_reduce_fusion = (f32[960]{0:T(1024)}, f32[2,256]{1,0:T(2,128)S(1)}, f32[2,256]{1,0:T(2,128)S(1)}, f32[960]{0:T(1024)}, f32[2,256,960]{1,2,0:T(8,128)}) fusion(f32[2,256,960]{1,2,0:T(8,128)} %get-tuple-element.53, f32[2,256]{1,0:T(2,128)S(1)} %get-tuple-element.90, f32[960]{0:T(1024)S(1)} %bitcast.340, f32[2,256,960]{1,2,0:T(8,128)} %get-tuple-element.31, ...), kind=kOutput, calls=%fused_computation.116 | convolution fusion | flops 5049545728 | bytes 22957312 | tf_op jit(solution)/shard_map/dot_general | solution.py:66
  399.2 24.1 %fusion = (f32[2,5,3,256]{3,2,1,0:T(4,128)S(1)}, f32[2,5,1024,256,3]{3,2,4,1,0:T(8,128)}) fusion(f32[2,5,1024,256,3]{3,2,4,1,0:T(8,128)} %get-tuple-element.100, f32[2,5,3,256]{3,2,1,0:T(4,128)S(1)} %log_add_fusion, bf16[2,256,5,3,64]{1,4,3,2,0:T(8,128)(2,1)S(1)} %bitcast.312, bf16[2,1024,5,64]{1,3,2,0:T(8,128)(2,1)S(1)} %copy-done.26), kind=kOutput, calls=%fused_computation.2 | convolution fusion | flops 1030218240 | bytes 65269760 | tf_op jit(solution)/shard_map/bqgrh,bkgh->bgrqk/dot_general | solution.py:187
  423.3 26.8 %fusion.2 = bf16[2,5,3,256,1024]{3,4,2,1,0:T(8,128)(2,1)} fusion(f32[2,5,1024,256,3]{3,2,4,1,0:T(8,128)} %get-tuple-element.106, f32[2,5,1024,256,3]{3,2,4,1,0:T(8,128)} %get-tuple-element.100, f32[2,5,3,256]{3,2,1,0:T(4,128)S(1)} %get-tuple-element.105, f32[2,5,3,256]{3,2,1,0:T(4,128)S(1)} %log_add_fusion), kind=kLoop, calls=%fused_computation.4 | loop fusion | flops 31457280 | bytes 78704640 | tf_op jit(solution)/shard_map/convert_element_type | solution.py:190
  450.1 11.4 %fusion.81 = bf16[2,1024,5,64]{1,3,2,0:T(8,128)(2,1)} fusion(bf16[2,5,3,256,1024]{3,4,2,1,0:T(8,128)(2,1)} %fusion.2, bf16[2,256,5,3,32]{1,4,3,2,0:T(8,128)(2,1)S(1)} %bitcast.323, bf16[2,256,5,3,32]{1,4,3,2,0:T(8,128)(2,1)S(1)} %bitcast.325), kind=kOutput, calls=%fused_computation.149 | convolution fusion | flops 1009909760 | bytes 18022400 | tf_op jit(solution)/shard_map/bgrqk,bqgrh->bkgh/dot_general | solution.py:198
  464.7 24.4 %fusion.3 = (f32[2,5,3,256]{3,2,1,0:T(4,128)S(1)}, f32[2,5,1024,256,3]{3,2,4,1,0:T(8,128)}) fusion(f32[2,5,1024,256,3]{3,2,4,1,0:T(8,128)} %get-tuple-element.102, f32[2,5,3,256]{3,2,1,0:T(4,128)S(1)} %copy-done.30, bf16[2,256,5,3,64]{1,4,3,2,0:T(8,128)(2,1)S(1)} %bitcast.310, bf16[2,1024,5,64]{1,3,2,0:T(8,128)(2,1)S(1)} %copy-done.25), kind=kOutput, calls=%fused_computation.7 | convolution fusion | flops 1030218240 | bytes 65269760 | tf_op jit(solution)/shard_map/bqgrh,bkgh->bgrqk/dot_general | solution.py:187
  489.1 26.6 %fusion.5 = bf16[2,5,3,256,1024]{3,4,2,1,0:T(8,128)(2,1)} fusion(f32[2,5,1024,256,3]{3,2,4,1,0:T(8,128)} %get-tuple-element.108, f32[2,5,1024,256,3]{3,2,4,1,0:T(8,128)} %get-tuple-element.102, f32[2,5,3,256]{3,2,1,0:T(4,128)S(1)} %get-tuple-element.107, f32[2,5,3,256]{3,2,1,0:T(4,128)S(1)} %copy-done.30), kind=kLoop, calls=%fused_computation.9 | loop fusion | flops 31457280 | bytes 78704640 | tf_op jit(solution)/shard_map/convert_element_type | solution.py:190
  515.7 11.5 %fusion.80 = bf16[2,1024,5,64]{1,3,2,0:T(8,128)(2,1)} fusion(bf16[2,5,3,256,1024]{3,4,2,1,0:T(8,128)(2,1)} %fusion.5, bf16[2,256,5,3,32]{1,4,3,2,0:T(8,128)(2,1)} %bitcast.321, bf16[2,256,5,3,32]{1,4,3,2,0:T(8,128)(2,1)S(1)} %bitcast.319), kind=kOutput, calls=%fused_computation.148 | convolution fusion | flops 1009909760 | bytes 18022400 | tf_op jit(solution)/shard_map/bgrqk,bqgrh->bkgh/dot_general | solution.py:198
  527.3 14.8 %fusion.77 = bf16[2,1024,5,64]{1,3,2,0:T(8,128)(2,1)} fusion(bf16[2,256,5,3,64]{1,4,3,2,0:T(8,128)(2,1)} %bitcast.313, f32[2,5,1024,256,3]{3,2,4,1,0:T(8,128)} %get-tuple-element.100, f32[2,5,3,256]{3,2,1,0:T(4,128)S(1)} %log_add_fusion), kind=kOutput, calls=%fused_computation.147 | convolution fusion | flops 1023016960 | bytes 33781760 | tf_op jit(solution)/shard_map/bgrqk,bqgrh->bkgh/dot_general | solution.py:203
  570.1 14.1 %fusion.74 = bf16[2,1024,5,64]{1,3,2,0:T(8,128)(2,1)} fusion(bf16[2,256,5,3,64]{1,4,3,2,0:T(8,128)(2,1)S(1)} %bitcast.311, f32[2,5,1024,256,3]{3,2,4,1,0:T(8,128)} %get-tuple-element.102, f32[2,5,3,256]{3,2,1,0:T(4,128)S(1)} %copy-done.30), kind=kOutput, calls=%fused_computation.146 | convolution fusion | flops 1023016960 | bytes 33781760 | tf_op jit(solution)/shard_map/bgrqk,bqgrh->bkgh/dot_general | solution.py:203
  608.3 35.2 %all-to-all-done.4 = bf16[960,8,4,80]{0,3,1,2:T(8,128)(2,1)} async-done(((bf16[960,8,4,80]{0,3,1,2:T(8,128)(2,1)}), bf16[960,8,4,80]{0,3,1,2:T(8,128)(2,1)}, u32[]{:S(2)}, u32[]{:S(2)}) %all-to-all-start.4) | async-done | bytes 4915232 | tf_op jit(solution)/shard_map/all_to_all | solution.py:253
  700.1 12.3 %fusion.41 = f32[960,5120,1]{1,0,2:T(8,128)} fusion(bf16[2,256,2560]{2,1,0:T(8,128)(2,1)} %get-tuple-element.37, bf16[2,256,2560]{2,1,0:T(8,128)(2,1)} %copy-done.95, f32[2,256,960]{1,2,0:T(8,128)} %get-tuple-element.31, f32[960]{0:T(1024)S(1)} %bitcast.342, f32[2,256]{1,0:T(2,128)S(1)} %copy-done.56), kind=kOutput, calls=%fused_computation.84 | convolution fusion | flops 5045125120 | bytes 26875648 | tf_op jit(solution)/shard_map/dot_general | solution.py:60
  712.4 13.8 %fusion.14 = bf16[960,5120]{1,0:T(8,128)(2,1)} fusion(f32[960,5120,1]{1,0,2:T(8,128)} %fusion.41, bf16[2,256,2560]{2,1,0:T(8,128)(2,1)} %get-tuple-element.35, bf16[2,256,2560]{2,1,0:T(8,128)(2,1)} %get-tuple-element.34, f32[2,256,960]{1,2,0:T(8,128)} %get-tuple-element.53, f32[2,256]{1,0:T(2,128)S(1)} %copy-done.60, f32[960]{0:T(1024)S(1)} %bitcast.343), kind=kOutput, calls=%fused_computation.29 | convolution fusion | flops 5054955520 | bytes 36706048 | tf_op jit(solution)/shard_map/dot_general | solution.py:60
  726.1 14.2 %copy.57 = bf16[960,5120]{0,1:T(8,128)(2,1)} copy(bf16[960,5120]{1,0:T(8,128)(2,1)} %fusion.14) | data formatting | bytes 19660800 | tf_op jit(solution)/shard_map/convert_element_type | solution.py:247
  740.4 9.9 copy.58
  770.6 110.4 %all-to-all-done.2 = bf16[960,8,4,160]{0,3,1,2:T(8,128)(2,1)} async-done(((bf16[960,8,4,160]{0,3,1,2:T(8,128)(2,1)}), bf16[960,8,4,160]{0,3,1,2:T(8,128)(2,1)}, u32[]{:S(2)}, u32[]{:S(2)}) %all-to-all-start.2) | async-done | bytes 9830432 | tf_op jit(solution)/shard_map/all_to_all | solution.py:246
  887.9 9.2 reduce_sum.271
  897.2 21.3 %all-to-all-done.1 = bf16[960,8,80]{0,2,1:T(8,128)(2,1)} async-done(((bf16[960,8,80]{0,2,1:T(8,128)(2,1)}), bf16[960,8,80]{0,2,1:T(8,128)(2,1)}, u32[]{:S(2)}, u32[]{:S(2)}) %all-to-all-start.1) | async-done | bytes 1228832 | tf_op jit(solution)/shard_map/all_to_all | solution.py:263
  938.1 63.9 %all-reduce = (f32[]{:T(128)}, f32[]{:T(128)}, f32[2,960]{1,0:T(2,128)}, f32[960]{0:T(1024)}) all-reduce(f32[]{:T(128)S(6)} %add.239, f32[]{:T(128)} %convert_reduce_fusion.3, f32[2,960]{1,0:T(2,128)S(1)} %pad_maximum_fusion.26, f32[960]{0:T(1024)S(1)} %add.263), channel_id=1, replica_groups=mesh['dp'=8,'ctx'=4] {'dp','ctx'}, use_global_device_ids=true, to_apply=%region_10.11 | all-reduce | flops 2882 | bytes 23056 | tf_op jit(solution)/shard_map/psum | solution.py:275
  (325 shorter events, 256.2 us)
Async XLA Ops:
  7.2 71.7 %copy-start = (bf16[4,256,960]{1,2,0:T(8,128)(2,1)S(1)}, bf16[4,256,960]{1,2,0:T(8,128)(2,1)}, u32[]{:S(2)}) copy-start(bf16[4,256,960]{1,2,0:T(8,128)(2,1)} %param.9) | copy-start | bytes 5898244
  7.2 71.7 %all-gather.8.cloned.1.call-start = ((), (), s32[]{:S(2)}) async-start(), calls=%async_computation.10 | async-start | bytes 5406720 | tf_op jit(solution)/shard_map/all_gather | solution.py:107
  7.9 102.6 %all-gather.20.cloned.1.call-start = ((), (), s32[]{:S(2)}) async-start(), calls=%async_computation.16 | async-start | bytes 1638400 | tf_op jit(solution)/shard_map/all_gather | solution.py:126
  10.5 72.5 %copy-start.75 = (f32[2,256]{1,0:T(2,128)}, f32[2,256]{1,0:T(2,128)S(1)}, u32[]{:S(2)}) copy-start(f32[2,256]{1,0:T(2,128)S(1)} %get-tuple-element.88) | copy-start | bytes 6148
  10.5 72.5 %copy-start.71 = (f32[2,256]{1,0:T(2,128)}, f32[2,256]{1,0:T(2,128)S(1)}, u32[]{:S(2)}) copy-start(f32[2,256]{1,0:T(2,128)S(1)} %get-tuple-element.110) | copy-start | bytes 6148
  10.5 72.5 %copy-start.49 = (f32[1,960]{1,0:T(1,128)}, f32[1,960]{1,0:T(1,128)S(1)}, u32[]{:S(2)}) copy-start(f32[1,960]{1,0:T(1,128)S(1)} %get-tuple-element.71) | copy-start | bytes 11524
  10.5 379.4 %copy-start.44 = (f32[1,960]{1,0:T(1,128)}, f32[1,960]{1,0:T(1,128)S(1)}, u32[]{:S(2)}) copy-start(f32[1,960]{1,0:T(1,128)S(1)} %get-tuple-element.70) | copy-start | bytes 11524
  10.7 96.1 %copy-start.38 = (f32[256,32]{0,1:T(8,128)}, f32[256,32]{0,1:T(8,128)S(1)}, u32[]{:S(2)}) copy-start(f32[256,32]{0,1:T(8,128)S(1)} %get-tuple-element.95) | copy-start | bytes 98308
  10.8 96.1 %copy-start.40 = (f32[256,32]{0,1:T(8,128)}, f32[256,32]{0,1:T(8,128)S(1)}, u32[]{:S(2)}) copy-start(f32[256,32]{0,1:T(8,128)S(1)} %get-tuple-element.96) | copy-start | bytes 98308
  87.7 50.7 %all-gather.12.cloned.1.call-start = ((), (), s32[]{:S(2)}) async-start(), calls=%async_computation.12 | async-start | bytes 1638400 | tf_op jit(solution)/shard_map/all_gather | solution.py:126
  88.5 77.4 %all-gather.18.cloned.1.call-start = ((), (), s32[]{:S(2)}) async-start(), calls=%async_computation.15 | async-start | bytes 1638400 | tf_op jit(solution)/shard_map/all_gather | solution.py:127
  90.5 93.2 %all-gather.10.cloned.1.call-start = ((), (), s32[]{:S(2)}) async-start(), calls=%async_computation.11 | async-start | bytes 1638400 | tf_op jit(solution)/shard_map/all_gather | solution.py:127
  92.4 161.9 %all-gather.14.cloned.1.call-start = ((), (), s32[]{:S(2)}) async-start(), calls=%async_computation.13 | async-start | bytes 10813440 | tf_op jit(solution)/shard_map/all_gather | solution.py:108
  93.0 228.0 %all-gather.16.cloned.1.call-start = ((), (), s32[]{:S(2)}) async-start(), calls=%async_computation.14 | async-start | bytes 5406720 | tf_op jit(solution)/shard_map/all_gather | solution.py:109
  93.7 564.2 %reduce-scatter.9.cloned.1.call-start = ((), (), s32[]{:S(2)}) async-start(), calls=%async_computation.19 | async-start | bytes 1638400 | tf_op jit(solution)/shard_map/reduce_scatter | solution.py:210
  203.0 187.0 %copy-start.53 = (f32[2,256]{1,0:T(2,128)}, f32[2,256]{1,0:T(2,128)S(1)}, u32[]{:S(2)}) copy-start(f32[2,256]{1,0:T(2,128)S(1)} %get-tuple-element.91) | copy-start | bytes 6148
  203.0 187.0 %copy-start.55 = (f32[2,256]{1,0:T(2,128)}, f32[2,256]{1,0:T(2,128)S(1)}, u32[]{:S(2)}) copy-start(f32[2,256]{1,0:T(2,128)S(1)} %get-tuple-element.92) | copy-start | bytes 6148
  203.0 187.0 %copy-start.57 = (f32[2,256]{1,0:T(2,128)}, f32[2,256]{1,0:T(2,128)S(1)}, u32[]{:S(2)}) copy-start(f32[2,256]{1,0:T(2,128)S(1)} %get-tuple-element.89) | copy-start | bytes 6148
  203.0 187.0 %copy-start.59 = (f32[2,256]{1,0:T(2,128)}, f32[2,256]{1,0:T(2,128)S(1)}, u32[]{:S(2)}) copy-start(f32[2,256]{1,0:T(2,128)S(1)} %get-tuple-element.90) | copy-start | bytes 6148
  461.5 198.3 %reduce-scatter.5.cloned.1.call-start = ((), (), s32[]{:S(2)}) async-start(), calls=%async_computation.17 | async-start | bytes 1638400 | tf_op jit(solution)/shard_map/reduce_scatter | solution.py:210
  527.3 136.5 %reduce-scatter.11.cloned.1.call-start = ((), (), s32[]{:S(2)}) async-start(), calls=%async_computation.20 | async-start | bytes 1638400 | tf_op jit(solution)/shard_map/reduce_scatter | solution.py:213
  564.9 78.5 %all-to-all-start.4 = ((bf16[960,8,4,80]{0,3,1,2:T(8,128)(2,1)}), bf16[960,8,4,80]{0,3,1,2:T(8,128)(2,1)}, u32[]{:S(2)}, u32[]{:S(2)}) async-start(bf16[960,8,4,80]{0,3,1,2:T(8,128)(2,1)} %copy.61), calls=%async_computation.8 | async-start | bytes 10485760 | tf_op jit(solution)/shard_map/all_to_all | solution.py:253
  570.0 99.9 %reduce-scatter.7.cloned.1.call-start = ((), (), s32[]{:S(2)}) async-start(), calls=%async_computation.18 | async-start | bytes 1638400 | tf_op jit(solution)/shard_map/reduce_scatter | solution.py:213
  648.7 46.1 %all-to-all-start.5 = ((bf16[960,8,80]{0,2,1:T(8,128)(2,1)}), bf16[960,8,80]{0,2,1:T(8,128)(2,1)S(1)}, u32[]{:S(2)}, u32[]{:S(2)}) async-start(bf16[960,8,80]{0,2,1:T(8,128)(2,1)} %reduce_sum.273), calls=%async_computation.9 | async-start | bytes 2621440 | tf_op jit(solution)/shard_map/all_to_all | solution.py:269
  694.8 64.7 %all-to-all-start = ((bf16[960,8,4,80]{0,3,1,2:T(8,128)(2,1)}), bf16[960,8,4,80]{0,3,1,2:T(8,128)(2,1)}, u32[]{:S(2)}, u32[]{:S(2)}) async-start(bf16[960,8,4,80]{0,3,1,2:T(8,128)(2,1)} %copy.55), calls=%async_computation.4 | async-start | bytes 10485760 | tf_op jit(solution)/shard_map/all_to_all | solution.py:239
  759.5 121.6 %all-to-all-start.2 = ((bf16[960,8,4,160]{0,3,1,2:T(8,128)(2,1)}), bf16[960,8,4,160]{0,3,1,2:T(8,128)(2,1)}, u32[]{:S(2)}, u32[]{:S(2)}) async-start(bf16[960,8,4,160]{0,3,1,2:T(8,128)(2,1)} %copy.58), calls=%async_computation.6 | async-start | bytes 20971520 | tf_op jit(solution)/shard_map/all_to_all | solution.py:246
  770.6 116.7 %copy-start.70 = (s32[4,256]{1,0:T(4,128)S(1)}, s32[4,256]{1,0:T(4,128)}, u32[]{:S(2)}) copy-start(s32[4,256]{1,0:T(4,128)} %param.11) | copy-start | bytes 12292
  881.0 37.4 %all-to-all-start.1 = ((bf16[960,8,80]{0,2,1:T(8,128)(2,1)}), bf16[960,8,80]{0,2,1:T(8,128)(2,1)}, u32[]{:S(2)}, u32[]{:S(2)}) async-start(bf16[960,8,80]{0,2,1:T(8,128)(2,1)} %reduce_sum.269), calls=%async_computation.5 | async-start | bytes 2621440 | tf_op jit(solution)/shard_map/all_to_all | solution.py:263
  918.4 97.5 %all-to-all-start.3 = ((bf16[960,8,160]{0,2,1:T(8,128)(2,1)}), bf16[960,8,160]{0,2,1:T(8,128)(2,1)}, u32[]{:S(2)}, u32[]{:S(2)}) async-start(bf16[960,8,160]{0,2,1:T(8,128)(2,1)} %reduce_sum.271), calls=%async_computation.7 | async-start | bytes 5242880 | tf_op jit(solution)/shard_map/all_to_all | solution.py:266
  936.6 66.7 %copy-start.47 = (f32[960]{0:T(1024)S(1)}, f32[960]{0:T(1024)}, u32[]{:S(2)}) copy-start(f32[960]{0:T(1024)} %param.17) | copy-start | bytes 11524
  936.6 66.7 %copy-start.58 = (f32[2,256]{1,0:T(2,128)S(1)}, f32[2,256]{1,0:T(2,128)}, u32[]{:S(2)}) copy-start(f32[2,256]{1,0:T(2,128)} %copy-done.57) | copy-start | bytes 6148
  936.6 66.7 %copy-start.64 = (f32[2,256]{1,0:T(2,128)S(1)}, f32[2,256]{1,0:T(2,128)}, u32[]{:S(2)}) copy-start(f32[2,256]{1,0:T(2,128)} %copy-done.63) | copy-start | bytes 6148
  (86 other events, 814.3 us)
Sparse Core Ops, SparseCore 0:
  10.8 68.0 all-gather.7
  87.8 16.8 all-gather.19
  106.9 18.3 all-gather.11
  127.2 18.3 all-gather.17
  146.9 18.3 all-gather.9
  168.0 86.2 all-gather.13
  257.1 63.8 all-gather.15
  461.7 24.9 reduce-scatter.8
  527.4 24.9 reduce-scatter.4
  555.3 33.5 reduce-scatter.10
  591.5 33.5 reduce-scatter.6
where the time goes:
time: 1030 us
  matrix products  347 us (34%)
  waiting for transfers between devices  333 us (32%)
  other arithmetic  149 us (14%)
  blocking collectives  74.7 us (7%)
  local copies, waits for them, and re-layouts  71.1 us (7%)
  starting transfers between devices  31.9 us (3%)
  between operations  19.2 us (2%)
    all_to_all x1, waiting for transfers between devices, on_device(): lax.all_to_all(owner_layout(grad_gu).astype(jnp.bfloat16), 'ctx', split_a...  110 us
    all_gather x1, waiting for transfers between devices, on_device(): lax.all_gather(packs[0], ('dp', 'ctx'), axis=1, tiled=True)  68.1 us
    dot_general x8, matrix products, by_columns(): lax.dot_general(left, right, (((2,), (1,)), ((), ())), preferred_element_...  67.6 us
    psum x1, blocking collectives, on_device(): lax.psum((energy, grad_gains, grad_router), ('dp', 'ctx'))  63.9 us
    convert_element_type x2, other arithmetic, on_device(): (probs * (d_probs - jnp.sum(probs * d_probs, axis=-1, keepdims=True))).as...  53.3 us
    dot_general x8, matrix products, over_rows(): lax.dot_general(left, right, (((0, 1), (0, 1)), ((), ())), preferred_elem...  51 us
    all_gather x1, waiting for transfers between devices, on_device(): lax.all_gather(packs[1], ('dp', 'ctx'), axis=1, tiled=True)  50.6 us
    dot_general x2, matrix products, on_device(): jnp.einsum('bqgrh,bkgh->bgrqk', d_heads_low, values_all, preferred_elemen...  48.6 us
  transfers between devices with their start and end apart: 17, of which 7 were waited for; matrix products, arithmetic and copies ran while one was open for 39% of the time, Pallas kernels for 0%

commit v1 on v0

--- a/solution.py
+++ b/solution.py
@@ -11,6 +11,18 @@
 MICRO = 2
 EPS = 1e-05
 THETA = 10000.0
+
+
+def doubled_up(x, axis, dim):
+    ways, here = (lax.axis_size(axis), lax.axis_index(axis))
+    grown, reach = (x, 1)
+    while reach < ways:
+        theirs = lax.ppermute(grown, axis, [(d, d ^ reach) for d in range(ways)])
+        mine_first = jnp.concatenate([grown, theirs], axis=dim)
+        theirs_first = jnp.concatenate([theirs, grown], axis=dim)
+        grown = jnp.where(here & reach == 0, mine_first, theirs_first)
+        reach = 2 * reach
+    return grown
 
 
 def shortened(x):
@@ -106,7 +118,7 @@
         fresh = (
             lax.all_gather(packs[0], ("dp", "ctx"), axis=1, tiled=True),
             lax.all_gather(packs[1], ("dp", "ctx"), axis=1, tiled=True),
-            lax.all_gather(packs[2], ("dp", "ctx"), axis=1, tiled=True),
+            doubled_up(packs[2], ("dp", "ctx"), 1),
         )
         w_attn, w_gu, w_down = fresh
         inv_one = lax.rsqrt(jnp.mean(x_float * x_float, axis=-1, keepdims=True) + EPS)

time: 1030 us -> 1120 us (1.087)
  waiting for transfers between devices: 333 us -> 403 us
  local copies, waits for them, and re-layouts: 71.1 us -> 86.8 us
    ppermute x0 -> x5, waiting for transfers between devices: none -> 157 us  [doubled_up(): theirs = lax.ppermute(grown, axis, [(d, d ^ reach) for d in range(ways)])]
    all_gather x1, waiting for transfers between devices: 50.6 us -> 0.01 us  [on_device(): lax.all_gather(packs[1], ('dp', 'ctx'), axis=1, tiled=True)]
    all_gather x1, waiting for transfers between devices: 36.5 us -> 0.01 us  [on_device(): lax.all_gather(packs[2], ('dp', 'ctx'), axis=1, tiled=True)]
  transfers between devices with their start and end apart: 17 -> 22, of which waited for: 7 -> 10; matrix products, arithmetic and copies ran while one was open for 39% -> 39% of each run, Pallas kernels for 0% -> 0%
where the time goes in v1:
time: 1120 us
  waiting for transfers between devices  403 us (36%)
  matrix products  337 us (30%)
  other arithmetic  156 us (14%)
  local copies, waits for them, and re-layouts  86.8 us (8%)
  blocking collectives  73.8 us (7%)
  starting transfers between devices  40.3 us (4%)
  between operations  19.2 us (2%)
    ppermute x5, waiting for transfers between devices, doubled_up(): theirs = lax.ppermute(grown, axis, [(d, d ^ reach) for d in range(ways)])  157 us
    all_to_all x1, waiting for transfers between devices, on_device(): lax.all_to_all(owner_layout(grad_gu).astype(jnp.bfloat16), 'ctx', split_a...  110 us
    all_gather x1, waiting for transfers between devices, on_device(): lax.all_gather(packs[0], ('dp', 'ctx'), axis=1, tiled=True)  66.3 us
    psum x1, blocking collectives, on_device(): lax.psum((energy, grad_gains, grad_router), ('dp', 'ctx'))  63.5 us
    dot_general x8, matrix products, by_columns(): lax.dot_general(left, right, (((2,), (1,)), ((), ())), preferred_element_...  61.8 us
    convert_element_type x2, other arithmetic, on_device(): (probs * (d_probs - jnp.sum(probs * d_probs, axis=-1, keepdims=True))).as...  53.4 us
    dot_general x8, matrix products, over_rows(): lax.dot_general(left, right, (((0, 1), (0, 1)), ((), ())), preferred_elem...  52.1 us
    dot_general x2, matrix products, on_device(): jnp.einsum('bqgrh,bkgh->bgrqk', d_heads_low, values_all, preferred_elemen...  49.1 us
  transfers between devices with their start and end apart: 22, of which 10 were waited for; matrix products, arithmetic and copies ran while one was open for 39% of the time, Pallas kernels for 0%

profile of v1, /device:TPU:0, one launch (start us, length us, event | category | flops | bytes accessed | tf_op | source)
XLA Modules:
  0.0 1116.0 jit_solution(15309844608433362363)
XLA Ops:
  12.6 66.3 %all-gather.8.cloned.1.call-done = bf16[960,2560]{0,1:T(8,128)(2,1)} async-done(((bf16[960,80]{0,1:T(8,128)(2,1)}), bf16[960,2560]{0,1:T(8,128)(2,1)}) %all-gather.8.cloned.1.call-update) | async-done | bytes 4915216 | tf_op jit(solution)/shard_map/all_gather | solution.py:119
  96.5 13.8 %collective-permute-done.1 = bf16[960,160]{0,1:T(8,128)(2,1)S(1)} collective-permute-done((bf16[960,160]{0,1:T(8,128)(2,1)S(1)}, bf16[960,160]{0,1:T(8,128)(2,1)S(1)}, u32[]{:S(2)}, u32[]{:S(2)}) %collective-permute-start.1) | collective-permute-done | bytes 307232 | tf_op jit(solution)/shard_map/ppermute | solution.py:20
  112.1 15.2 %collective-permute-done.2 = bf16[960,320]{0,1:T(8,128)(2,1)} collective-permute-done((bf16[960,320]{0,1:T(8,128)(2,1)S(1)}, bf16[960,320]{0,1:T(8,128)(2,1)}, u32[]{:S(2)}, u32[]{:S(2)}) %collective-permute-start.2) | collective-permute-done | bytes 614432 | tf_op jit(solution)/shard_map/ppermute | solution.py:20
  132.5 26.8 %collective-permute-done.3 = bf16[960,640]{1,0:T(8,128)(2,1)} collective-permute-done((bf16[960,640]{1,0:T(8,128)(2,1)}, bf16[960,640]{1,0:T(8,128)(2,1)}, u32[]{:S(2)}, u32[]{:S(2)}) %collective-permute-start.3) | collective-permute-done | bytes 1228832 | tf_op jit(solution)/shard_map/ppermute | solution.py:20
  184.8 99.3 %collective-permute-done.4 = bf16[960,1280]{1,0:T(8,128)(2,1)} collective-permute-done((bf16[960,1280]{1,0:T(8,128)(2,1)}, bf16[960,1280]{1,0:T(8,128)(2,1)}, u32[]{:S(2)}, u32[]{:S(2)}) %collective-permute-start.4) | collective-permute-done | bytes 2457632 | tf_op jit(solution)/shard_map/ppermute | solution.py:20
  292.5 14.9 %bitcast_reduce_fusion = (f32[2,5,3,256]{3,2,1,0:T(4,128)S(1)}, f32[2,5,1024,256,3]{3,2,4,1,0:T(8,128)}) fusion(bf16[2,256,5,3,32]{1,4,3,2,0:T(8,128)(2,1)S(1)} %bitcast.321, bf16[2,256,5,3,32]{1,4,3,2,0:T(8,128)(2,1)} %bitcast.323, bf16[2,1024,5,64]{1,3,2,0:T(8,128)(2,1)} %all-gather.18.cloned.1.call-done, pred[2,1024]{1,0:T(4,128)(4,1)S(1)} %get-tuple-element.98), kind=kOutput, calls=%fused_computation.12 | convolution fusion | flops 1032184320 | bytes 33783808 | tf_op jit(solution)/shard_map/bqgrh,bkgh->bgrqk/dot_general | solution.py:66
  307.4 13.5 %fusion.11 = f32[2,5,3,256]{3,2,1,0:T(4,128)S(1)} fusion(f32[2,5,1024,256,3]{3,2,4,1,0:T(8,128)} %get-tuple-element.100, f32[2,5,3,256]{3,2,1,0:T(4,128)S(1)} %get-tuple-element.99), kind=kLoop, calls=%fused_computation.25 | loop fusion | flops 15720960 | bytes 31518720 | tf_op jit(solution)/shard_map/reduce_sum | solution.py:146
  321.0 14.4 %bitcast_reduce_fusion.1 = (f32[2,5,3,256]{3,2,1,0:T(4,128)S(1)}, f32[2,5,1024,256,3]{3,2,4,1,0:T(8,128)}) fusion(bf16[2,256,5,3,32]{1,4,3,2,0:T(8,128)(2,1)S(1)} %bitcast.319, bf16[2,256,5,3,32]{1,4,3,2,0:T(8,128)(2,1)S(1)} %bitcast.317, bf16[2,1024,5,64]{1,3,2,0:T(8,128)(2,1)} %all-gather.12.cloned.1.call-done, pred[2,1024]{1,0:T(4,128)(4,1)S(1)} %get-tuple-element.97), kind=kOutput, calls=%fused_computation.17 | convolution fusion | flops 1032184320 | bytes 33783808 | tf_op jit(solution)/shard_map/bqgrh,bkgh->bgrqk/dot_general | solution.py:66
  335.4 13.1 %fusion.10 = f32[2,5,3,256]{3,2,1,0:T(4,128)S(1)} fusion(f32[2,5,1024,256,3]{3,2,4,1,0:T(8,128)} %get-tuple-element.102, f32[2,5,3,256]{3,2,1,0:T(4,128)S(1)} %get-tuple-element.101), kind=kLoop, calls=%fused_computation.24 | loop fusion | flops 15720960 | bytes 31518720 | tf_op jit(solution)/shard_map/reduce_sum | solution.py:146
  348.5 13.3 %fusion.73 = bf16[2,5,64,3,256]{4,2,3,1,0:T(8,128)(2,1)S(1)} fusion(f32[2,5,1024,256,3]{3,2,4,1,0:T(8,128)} %get-tuple-element.100, f32[2,5,3,256]{3,2,1,0:T(4,128)S(1)} %fusion.11, f32[2,5,3,256]{3,2,1,0:T(4,128)S(1)} %get-tuple-element.99, bf16[2,1024,5,64]{1,3,2,0:T(8,128)(2,1)} %all-gather.16.cloned.1.call-done), kind=kOutput, calls=%fused_computation.145 | convolution fusion | flops 1030717440 | bytes 33812480 | tf_op jit(solution)/shard_map/bgrqk,bkgh->bqgrh/dot_general | solution.py:149
  361.9 13.5 %fusion.74 = bf16[2,5,64,3,256]{4,2,3,1,0:T(8,128)(2,1)S(1)} fusion(f32[2,5,1024,256,3]{3,2,4,1,0:T(8,128)} %get-tuple-element.102, f32[2,5,3,256]{3,2,1,0:T(4,128)S(1)} %fusion.10, f32[2,5,3,256]{3,2,1,0:T(4,128)S(1)} %get-tuple-element.101, bf16[2,1024,5,64]{1,3,2,0:T(8,128)(2,1)} %all-gather.10.cloned.1.call-done), kind=kOutput, calls=%fused_computation.146 | convolution fusion | flops 1030717440 | bytes 33812480 | tf_op jit(solution)/shard_map/bgrqk,bkgh->bqgrh/dot_general | solution.py:149
  385.4 9.5 fusion.29
  407.1 9.4 fusion.27
  421.7 9.9 multiply_reduce_fusion.3
  451.1 10.6 fusion.25
  461.7 14.9 %multiply_reduce_fusion = (f32[960]{0:T(1024)}, f32[2,256]{1,0:T(2,128)S(1)}, f32[2,256]{1,0:T(2,128)S(1)}, f32[960]{0:T(1024)}, f32[2,256,960]{1,2,0:T(8,128)}) fusion(f32[2,256,960]{1,2,0:T(8,128)} %get-tuple-element.53, f32[2,256]{1,0:T(2,128)S(1)} %get-tuple-element.90, f32[960]{0:T(1024)S(1)} %bitcast.339, f32[2,256,960]{1,2,0:T(8,128)} %get-tuple-element.31, ...), kind=kOutput, calls=%fused_computation.117 | convolution fusion | flops 5049545728 | bytes 22957312 | tf_op jit(solution)/shard_map/dot_general | solution.py:78
  486.0 24.3 %fusion = (f32[2,5,3,256]{3,2,1,0:T(4,128)S(1)}, f32[2,5,1024,256,3]{3,2,4,1,0:T(8,128)}) fusion(f32[2,5,1024,256,3]{3,2,4,1,0:T(8,128)} %get-tuple-element.100, f32[2,5,3,256]{3,2,1,0:T(4,128)S(1)} %log_add_fusion, bf16[2,256,5,3,64]{1,4,3,2,0:T(8,128)(2,1)S(1)} %bitcast.311, bf16[2,1024,5,64]{1,3,2,0:T(8,128)(2,1)S(1)} %copy-done.28), kind=kOutput, calls=%fused_computation.2 | convolution fusion | flops 1030218240 | bytes 65269760 | tf_op jit(solution)/shard_map/bqgrh,bkgh->bgrqk/dot_general | solution.py:199
  510.3 26.8 %fusion.2 = bf16[2,5,3,256,1024]{3,4,2,1,0:T(8,128)(2,1)} fusion(f32[2,5,1024,256,3]{3,2,4,1,0:T(8,128)} %get-tuple-element.106, f32[2,5,1024,256,3]{3,2,4,1,0:T(8,128)} %get-tuple-element.100, f32[2,5,3,256]{3,2,1,0:T(4,128)S(1)} %get-tuple-element.105, f32[2,5,3,256]{3,2,1,0:T(4,128)S(1)} %log_add_fusion), kind=kLoop, calls=%fused_computation.4 | loop fusion | flops 31457280 | bytes 78704640 | tf_op jit(solution)/shard_map/convert_element_type | solution.py:202
  537.1 11.4 %fusion.82 = bf16[2,1024,5,64]{1,3,2,0:T(8,128)(2,1)} fusion(bf16[2,5,3,256,1024]{3,4,2,1,0:T(8,128)(2,1)} %fusion.2, bf16[2,256,5,3,32]{1,4,3,2,0:T(8,128)(2,1)S(1)} %bitcast.322, bf16[2,256,5,3,32]{1,4,3,2,0:T(8,128)(2,1)S(1)} %bitcast.324), kind=kOutput, calls=%fused_computation.150 | convolution fusion | flops 1009909760 | bytes 18022400 | tf_op jit(solution)/shard_map/bgrqk,bqgrh->bkgh/dot_general | solution.py:210
  551.7 24.9 %fusion.3 = (f32[2,5,3,256]{3,2,1,0:T(4,128)S(1)}, f32[2,5,1024,256,3]{3,2,4,1,0:T(8,128)}) fusion(f32[2,5,1024,256,3]{3,2,4,1,0:T(8,128)} %get-tuple-element.102, f32[2,5,3,256]{3,2,1,0:T(4,128)S(1)} %copy-done.34, bf16[2,256,5,3,64]{1,4,3,2,0:T(8,128)(2,1)S(1)} %bitcast.309, bf16[2,1024,5,64]{1,3,2,0:T(8,128)(2,1)S(1)} %copy-done.27), kind=kOutput, calls=%fused_computation.7 | convolution fusion | flops 1030218240 | bytes 65269760 | tf_op jit(solution)/shard_map/bqgrh,bkgh->bgrqk/dot_general | solution.py:199
  576.5 26.6 %fusion.5 = bf16[2,5,3,256,1024]{3,4,2,1,0:T(8,128)(2,1)} fusion(f32[2,5,1024,256,3]{3,2,4,1,0:T(8,128)} %get-tuple-element.108, f32[2,5,1024,256,3]{3,2,4,1,0:T(8,128)} %get-tuple-element.102, f32[2,5,3,256]{3,2,1,0:T(4,128)S(1)} %get-tuple-element.107, f32[2,5,3,256]{3,2,1,0:T(4,128)S(1)} %copy-done.34), kind=kLoop, calls=%fused_computation.9 | loop fusion | flops 31457280 | bytes 78704640 | tf_op jit(solution)/shard_map/convert_element_type | solution.py:202
  603.1 11.5 %fusion.81 = bf16[2,1024,5,64]{1,3,2,0:T(8,128)(2,1)} fusion(bf16[2,5,3,256,1024]{3,4,2,1,0:T(8,128)(2,1)} %fusion.5, bf16[2,256,5,3,32]{1,4,3,2,0:T(8,128)(2,1)} %bitcast.320, bf16[2,256,5,3,32]{1,4,3,2,0:T(8,128)(2,1)S(1)} %bitcast.318), kind=kOutput, calls=%fused_computation.149 | convolution fusion | flops 1009909760 | bytes 18022400 | tf_op jit(solution)/shard_map/bgrqk,bqgrh->bkgh/dot_general | solution.py:210
  614.7 14.5 %fusion.78 = bf16[2,1024,5,64]{1,3,2,0:T(8,128)(2,1)} fusion(bf16[2,256,5,3,64]{1,4,3,2,0:T(8,128)(2,1)} %bitcast.312, f32[2,5,1024,256,3]{3,2,4,1,0:T(8,128)} %get-tuple-element.100, f32[2,5,3,256]{3,2,1,0:T(4,128)S(1)} %log_add_fusion), kind=kOutput, calls=%fused_computation.148 | convolution fusion | flops 1023016960 | bytes 33781760 | tf_op jit(solution)/shard_map/bgrqk,bqgrh->bkgh/dot_general | solution.py:215
  657.1 14.4 %fusion.75 = bf16[2,1024,5,64]{1,3,2,0:T(8,128)(2,1)} fusion(bf16[2,256,5,3,64]{1,4,3,2,0:T(8,128)(2,1)S(1)} %bitcast.310, f32[2,5,1024,256,3]{3,2,4,1,0:T(8,128)} %get-tuple-element.102, f32[2,5,3,256]{3,2,1,0:T(4,128)S(1)} %copy-done.34), kind=kOutput, calls=%fused_computation.147 | convolution fusion | flops 1023016960 | bytes 33781760 | tf_op jit(solution)/shard_map/bgrqk,bqgrh->bkgh/dot_general | solution.py:215
  693.0 37.5 %all-to-all-done.4 = bf16[960,8,4,80]{0,3,1,2:T(8,128)(2,1)} async-done(((bf16[960,8,4,80]{0,3,1,2:T(8,128)(2,1)}), bf16[960,8,4,80]{0,3,1,2:T(8,128)(2,1)}, u32[]{:S(2)}, u32[]{:S(2)}) %all-to-all-start.4) | async-done | bytes 4915232 | tf_op jit(solution)/shard_map/all_to_all | solution.py:265
  788.9 12.3 %fusion.38 = f32[960,5120,1]{1,0,2:T(8,128)} fusion(bf16[2,256,2560]{2,1,0:T(8,128)(2,1)} %copy-done.97, bf16[2,256,2560]{2,1,0:T(8,128)(2,1)} %copy-done.96, f32[2,256,960]{1,2,0:T(8,128)} %get-tuple-element.31, f32[960]{0:T(1024)S(1)} %bitcast.341, f32[2,256]{1,0:T(2,128)S(1)} %copy-done.59), kind=kOutput, calls=%fused_computation.82 | convolution fusion | flops 5045125120 | bytes 26875648 | tf_op jit(solution)/shard_map/dot_general | solution.py:72
  801.2 13.7 %fusion.14 = bf16[960,5120]{1,0:T(8,128)(2,1)} fusion(f32[960,5120,1]{1,0,2:T(8,128)} %fusion.38, bf16[2,256,2560]{2,1,0:T(8,128)(2,1)} %get-tuple-element.35, bf16[2,256,2560]{2,1,0:T(8,128)(2,1)} %get-tuple-element.34, f32[2,256,960]{1,2,0:T(8,128)} %get-tuple-element.53, f32[2,256]{1,0:T(2,128)S(1)} %copy-done.63, f32[960]{0:T(1024)S(1)} %bitcast.342), kind=kOutput, calls=%fused_computation.29 | convolution fusion | flops 5054955520 | bytes 36706048 | tf_op jit(solution)/shard_map/dot_general | solution.py:72
  814.9 14.3 %copy.93 = bf16[960,5120]{0,1:T(8,128)(2,1)} copy(bf16[960,5120]{1,0:T(8,128)(2,1)} %fusion.14) | data formatting | bytes 19660800 | tf_op jit(solution)/shard_map/convert_element_type | solution.py:259
  829.2 9.9 copy.94
  859.5 110.4 %all-to-all-done.2 = bf16[960,8,4,160]{0,3,1,2:T(8,128)(2,1)} async-done(((bf16[960,8,4,160]{0,3,1,2:T(8,128)(2,1)}), bf16[960,8,4,160]{0,3,1,2:T(8,128)(2,1)}, u32[]{:S(2)}, u32[]{:S(2)}) %all-to-all-start.2) | async-done | bytes 9830432 | tf_op jit(solution)/shard_map/all_to_all | solution.py:258
  986.3 21.2 %all-to-all-done.1 = bf16[960,8,80]{0,2,1:T(8,128)(2,1)} async-done(((bf16[960,8,80]{0,2,1:T(8,128)(2,1)}), bf16[960,8,80]{0,2,1:T(8,128)(2,1)}, u32[]{:S(2)}, u32[]{:S(2)}) %all-to-all-start.1) | async-done | bytes 1228832 | tf_op jit(solution)/shard_map/all_to_all | solution.py:275
  1027.5 63.5 %all-reduce = (f32[]{:T(128)}, f32[]{:T(128)}, f32[2,960]{1,0:T(2,128)}, f32[960]{0:T(1024)}) all-reduce(f32[]{:T(128)S(6)} %add.244, f32[]{:T(128)} %convert_reduce_fusion.3, f32[2,960]{1,0:T(2,128)S(1)} %pad_maximum_fusion.26, f32[960]{0:T(1024)S(1)} %add.268), channel_id=1, replica_groups=mesh['dp'=8,'ctx'=4] {'dp','ctx'}, use_global_device_ids=true, to_apply=%region_10.11 | all-reduce | flops 2882 | bytes 23056 | tf_op jit(solution)/shard_map/psum | solution.py:287
  (340 shorter events, 301.1 us)
Async XLA Ops:
  7.2 71.7 %all-gather.8.cloned.1.call-start = ((), (), s32[]{:S(2)}) async-start(), calls=%async_computation.10 | async-start | bytes 5406720 | tf_op jit(solution)/shard_map/all_gather | solution.py:119
  7.9 284.6 %all-gather.18.cloned.1.call-start = ((), (), s32[]{:S(2)}) async-start(), calls=%async_computation.15 | async-start | bytes 1638400 | tf_op jit(solution)/shard_map/all_gather | solution.py:138
  12.6 276.0 %copy-start.41 = (f32[256,32]{0,1:T(8,128)}, f32[256,32]{0,1:T(8,128)S(1)}, u32[]{:S(2)}) copy-start(f32[256,32]{0,1:T(8,128)S(1)} %get-tuple-element.95) | copy-start | bytes 98308
  12.6 276.0 %copy-start.43 = (f32[256,32]{0,1:T(8,128)}, f32[256,32]{0,1:T(8,128)S(1)}, u32[]{:S(2)}) copy-start(f32[256,32]{0,1:T(8,128)S(1)} %get-tuple-element.96) | copy-start | bytes 98308
  88.0 233.0 %all-gather.12.cloned.1.call-start = ((), (), s32[]{:S(2)}) async-start(), calls=%async_computation.12 | async-start | bytes 1638400 | tf_op jit(solution)/shard_map/all_gather | solution.py:138
  88.8 259.7 %all-gather.16.cloned.1.call-start = ((), (), s32[]{:S(2)}) async-start(), calls=%async_computation.14 | async-start | bytes 1638400 | tf_op jit(solution)/shard_map/all_gather | solution.py:139
  90.7 271.1 %all-gather.10.cloned.1.call-start = ((), (), s32[]{:S(2)}) async-start(), calls=%async_computation.11 | async-start | bytes 1638400 | tf_op jit(solution)/shard_map/all_gather | solution.py:139
  92.7 292.8 %all-gather.14.cloned.1.call-start = ((), (), s32[]{:S(2)}) async-start(), calls=%async_computation.13 | async-start | bytes 10813440 | tf_op jit(solution)/shard_map/all_gather | solution.py:120
  93.2 338.4 %all-gather.20.cloned.1.call-start = ((), (), s32[]{:S(2)}) async-start(), calls=%async_computation.16 | async-start | bytes 5406720 | tf_op jit(solution)/shard_map/all_gather | solution.py:173
  93.3 1.7 collective-permute-start
  95.1 15.3 %collective-permute-start.1 = (bf16[960,160]{0,1:T(8,128)(2,1)S(1)}, bf16[960,160]{0,1:T(8,128)(2,1)S(1)}, u32[]{:S(2)}, u32[]{:S(2)}) collective-permute-start(bf16[960,160]{0,1:T(8,128)(2,1)S(1)} %maximum_select_fusion.4), channel_id=1, source_target_pairs={{0,2},{1,3},{2,0},{3,1},{4,6},{5,7},{6,4},{7,5},{8,10},{9,11},{10,... | collective-permute-start | bytes 921608 | tf_op jit(solution)/shard_map/ppermute | solution.py:20
  110.6 16.7 %collective-permute-start.2 = (bf16[960,320]{0,1:T(8,128)(2,1)S(1)}, bf16[960,320]{0,1:T(8,128)(2,1)}, u32[]{:S(2)}, u32[]{:S(2)}) collective-permute-start(bf16[960,320]{0,1:T(8,128)(2,1)S(1)} %maximum_select_fusion.3), channel_id=1, source_target_pairs={{0,4},{1,5},{2,6},{3,7},{4,0},{5,1},{6,2},{7,3},{8,12},{9,13},{10,... | collective-permute-start | bytes 1843208 | tf_op jit(solution)/shard_map/ppermute | solution.py:20
  131.0 28.3 %collective-permute-start.3 = (bf16[960,640]{1,0:T(8,128)(2,1)}, bf16[960,640]{1,0:T(8,128)(2,1)}, u32[]{:S(2)}, u32[]{:S(2)}) collective-permute-start(bf16[960,640]{1,0:T(8,128)(2,1)} %copy.73), channel_id=1, source_target_pairs={{0,8},{1,9},{2,10},{3,11},{4,12},{5,13},{6,14},{7,15},{8,0},{9,1},... | collective-permute-start | bytes 3686408 | tf_op jit(solution)/shard_map/ppermute | solution.py:20
  169.9 114.3 %collective-permute-start.4 = (bf16[960,1280]{1,0:T(8,128)(2,1)}, bf16[960,1280]{1,0:T(8,128)(2,1)}, u32[]{:S(2)}, u32[]{:S(2)}) collective-permute-start(bf16[960,1280]{1,0:T(8,128)(2,1)} %copy.76), channel_id=1, source_target_pairs={{0,16},{1,17},{2,18},{3,19},{4,20},{5,21},{6,22},{7,23},{8,24},{9,... | collective-permute-start | bytes 7372808 | tf_op jit(solution)/shard_map/ppermute | solution.py:20
  172.2 574.4 %reduce-scatter.9.cloned.1.call-start = ((), (), s32[]{:S(2)}) async-start(), calls=%async_computation.19 | async-start | bytes 1638400 | tf_op jit(solution)/shard_map/reduce_scatter | solution.py:222
  172.3 116.3 %copy-start.54 = (f32[4,256]{1,0:T(4,128)}, f32[4,256]{1,0:T(4,128)S(1)}, u32[]{:S(2)}) copy-start(f32[4,256]{1,0:T(4,128)S(1)} %get-tuple-element.82) | copy-start | bytes 12292
  183.7 104.9 %copy-start.68 = (f32[1,2,256]{2,0,1:T(1,128)}, f32[1,2,256]{2,0,1:T(1,128)S(1)}, u32[]{:S(2)}) copy-start(f32[1,2,256]{2,0,1:T(1,128)S(1)} %fusion.145) | copy-start | bytes 6148
  184.2 104.4 %copy-start.70 = (f32[1,2,256]{2,0,1:T(1,128)}, f32[1,2,256]{2,0,1:T(1,128)S(1)}, u32[]{:S(2)}) copy-start(f32[1,2,256]{2,0,1:T(1,128)S(1)} %fusion.144) | copy-start | bytes 6148
  384.7 92.0 %copy-start.56 = (f32[2,256]{1,0:T(2,128)}, f32[2,256]{1,0:T(2,128)S(1)}, u32[]{:S(2)}) copy-start(f32[2,256]{1,0:T(2,128)S(1)} %get-tuple-element.91) | copy-start | bytes 6148
  384.7 92.0 %copy-start.58 = (f32[2,256]{1,0:T(2,128)}, f32[2,256]{1,0:T(2,128)S(1)}, u32[]{:S(2)}) copy-start(f32[2,256]{1,0:T(2,128)S(1)} %get-tuple-element.92) | copy-start | bytes 6148
  384.7 92.0 %copy-start.60 = (f32[2,256]{1,0:T(2,128)}, f32[2,256]{1,0:T(2,128)S(1)}, u32[]{:S(2)}) copy-start(f32[2,256]{1,0:T(2,128)S(1)} %get-tuple-element.89) | copy-start | bytes 6148
  384.7 92.0 %copy-start.62 = (f32[2,256]{1,0:T(2,128)}, f32[2,256]{1,0:T(2,128)S(1)}, u32[]{:S(2)}) copy-start(f32[2,256]{1,0:T(2,128)S(1)} %get-tuple-element.90) | copy-start | bytes 6148
  548.5 200.1 %reduce-scatter.5.cloned.1.call-start = ((), (), s32[]{:S(2)}) async-start(), calls=%async_computation.17 | async-start | bytes 1638400 | tf_op jit(solution)/shard_map/reduce_scatter | solution.py:222
  614.7 137.8 %reduce-scatter.11.cloned.1.call-start = ((), (), s32[]{:S(2)}) async-start(), calls=%async_computation.20 | async-start | bytes 1638400 | tf_op jit(solution)/shard_map/reduce_scatter | solution.py:225
  651.9 78.5 %all-to-all-start.4 = ((bf16[960,8,4,80]{0,3,1,2:T(8,128)(2,1)}), bf16[960,8,4,80]{0,3,1,2:T(8,128)(2,1)}, u32[]{:S(2)}, u32[]{:S(2)}) async-start(bf16[960,8,4,80]{0,3,1,2:T(8,128)(2,1)} %copy.97), calls=%async_computation.8 | async-start | bytes 10485760 | tf_op jit(solution)/shard_map/all_to_all | solution.py:265
  657.0 101.5 %reduce-scatter.7.cloned.1.call-start = ((), (), s32[]{:S(2)}) async-start(), calls=%async_computation.18 | async-start | bytes 1638400 | tf_op jit(solution)/shard_map/reduce_scatter | solution.py:225
  735.7 47.8 %all-to-all-start.5 = ((bf16[960,8,80]{0,2,1:T(8,128)(2,1)}), bf16[960,8,80]{0,2,1:T(8,128)(2,1)S(1)}, u32[]{:S(2)}, u32[]{:S(2)}) async-start(bf16[960,8,80]{0,2,1:T(8,128)(2,1)} %reduce_sum.273), calls=%async_computation.9 | async-start | bytes 2621440 | tf_op jit(solution)/shard_map/all_to_all | solution.py:281
  783.5 64.8 %all-to-all-start = ((bf16[960,8,4,80]{0,3,1,2:T(8,128)(2,1)}), bf16[960,8,4,80]{0,3,1,2:T(8,128)(2,1)}, u32[]{:S(2)}, u32[]{:S(2)}) async-start(bf16[960,8,4,80]{0,3,1,2:T(8,128)(2,1)} %copy.91), calls=%async_computation.4 | async-start | bytes 10485760 | tf_op jit(solution)/shard_map/all_to_all | solution.py:251
  848.3 121.6 %all-to-all-start.2 = ((bf16[960,8,4,160]{0,3,1,2:T(8,128)(2,1)}), bf16[960,8,4,160]{0,3,1,2:T(8,128)(2,1)}, u32[]{:S(2)}, u32[]{:S(2)}) async-start(bf16[960,8,4,160]{0,3,1,2:T(8,128)(2,1)} %copy.94), calls=%async_computation.6 | async-start | bytes 20971520 | tf_op jit(solution)/shard_map/all_to_all | solution.py:258
  859.5 116.9 %copy-start.73 = (s32[4,256]{1,0:T(4,128)S(1)}, s32[4,256]{1,0:T(4,128)}, u32[]{:S(2)}) copy-start(s32[4,256]{1,0:T(4,128)} %param.11) | copy-start | bytes 12292
  969.9 37.6 %all-to-all-start.1 = ((bf16[960,8,80]{0,2,1:T(8,128)(2,1)}), bf16[960,8,80]{0,2,1:T(8,128)(2,1)}, u32[]{:S(2)}, u32[]{:S(2)}) async-start(bf16[960,8,80]{0,2,1:T(8,128)(2,1)} %reduce_sum.269), calls=%async_computation.5 | async-start | bytes 2621440 | tf_op jit(solution)/shard_map/all_to_all | solution.py:275
  1007.5 97.4 %all-to-all-start.3 = ((bf16[960,8,160]{0,2,1:T(8,128)(2,1)}), bf16[960,8,160]{0,2,1:T(8,128)(2,1)}, u32[]{:S(2)}, u32[]{:S(2)}) async-start(bf16[960,8,160]{0,2,1:T(8,128)(2,1)} %reduce_sum.271), calls=%async_computation.7 | async-start | bytes 5242880 | tf_op jit(solution)/shard_map/all_to_all | solution.py:278
  (90 other events, 1264.2 us)
Sparse Core Ops, SparseCore 0:
  10.8 68.0 all-gather.7
  88.1 22.1 all-gather.17
  111.9 19.8 all-gather.11
  133.8 18.3 all-gather.15
  153.5 18.3 all-gather.9
  174.6 174.1 all-gather.13
  351.7 63.8 all-gather.19
  548.6 26.4 reduce-scatter.8
  614.8 26.5 reduce-scatter.4
  644.3 33.5 reduce-scatter.10
  680.5 33.6 reduce-scatter.6
